TPU v7x, 512 devices: a whole 4x8x8 slice. The times are simulated.
512 devices in a mesh: row: 32 (over z, x), col: 16 (over y, core).
Axes of the slice: x: 4, y: 8, z: 8, core: 2. Of those that a mesh axis runs over, the one named last changes fastest.
Arguments:
- rhs: float32 [512, 64, 128], P(('row', 'col')), may hold values from -16 to 16
- item_factors: bfloat16 [1024, 64, 128], P('col'), may hold values from -0.125 to 0.125
- slot_users: int32 [32, 16, 96], P('row', 'col'), may hold values from 0 to 15, as said below
- slot_items: int32 [32, 16, 96], P('row', 'col'), may hold values from 0 to 63
- slot_counts: int32 [32, 16], P('row', 'col'), may hold values from 12 to 96, as said below
- mask_words: int32 [32, 16, 96, 16, 128], P('row', 'col'), may hold values from 0 to 255
- self_tiles: int32 [512, 128, 128], P(('row', 'col')), may hold values from 0 to 3, as said below
- next_tiles: int32 [512, 128, 128], P(('row', 'col')), may hold values from 0 to 3, as said below
Outputs:
- solution: float32 [512, 64, 128], P(('row', 'col'))
- residual: float32 [512, 64, 128], P(('row', 'col'))
Inputs may be any that keep to these rules, and one draw needn't show every extreme that they name: `slot_users`: on each grid cell the 96 slots name distinct pairs of user block and item block. Some grid cells use all 96 slots; slots at positions slot_counts or later are ignored. `self_tiles`: most weights are zero. `next_tiles`: most weights are zero.
All inputs are finite; a program needn't handle non-finite values.
Results may differ from a plain program's by a relative error of at most 0.018.
Values may be sent and summed in bfloat16 or wider, within the bound.
A program may use at most 64 MiB of HBM per device.

v0:
```python
import jax
import jax.numpy as jnp
from jax import lax
from jax.sharding import Mesh
from jax.sharding import PartitionSpec as P

ITERS = 2
COL = ("col_0", "col_1")
ROW_COL = ("row_0", "row_1", "col_0", "col_1")
ROW = ("row_0", "row_1")


graph_weight = 0.01
ridge_weight = 0.5


def in_order(blocks, dim):
    blocks = jnp.moveaxis(blocks, 0, dim)
    lengths = blocks.shape
    return blocks.reshape(*lengths[:dim], lengths[dim] * lengths[dim + 1], *lengths[dim + 2 :])


def from_everyone(x, axis):
    size = lax.axis_size(axis)
    return lax.all_to_all(jnp.broadcast_to(x[None], (size, *x.shape)), axis, 0, 0, tiled=True)


def gathered_copies(x, axis, dim):
    return in_order(from_everyone(x, axis), dim)


def split_up(x, dim, size):
    lengths = x.shape
    blocks = x.reshape(*lengths[:dim], size, lengths[dim] // size, *lengths[dim + 1 :])
    return jnp.moveaxis(blocks, dim, 0)


def sum_at_owner(x, axis, dim):
    size = lax.axis_size(axis)
    blocks = lax.all_to_all(split_up(x, dim, size), axis, 0, 0, tiled=True)
    return jnp.sum(blocks, axis=0)


def one_axis_at_a_time(x, axes):
    for axis in axes:
        x = lax.psum(x, axis)
    return x


def group_size():
    return 16


def unpack_masks(words):
    shifts = jnp.arange(8, dtype=jnp.int32)
    bits = jnp.right_shift(words[:, :, None, :], shifts[None, None, :, None]) & 1
    return bits.reshape(words.shape[0], words.shape[1] * 8, words.shape[2]).astype(jnp.float32)


def masked_tiles(row_dir, item_factors, users, items, words, valid):
    scores = jnp.einsum(
        "sdi,sdu->siu", item_factors[items], row_dir[users], preferred_element_type=jnp.float32
    )
    return (scores * unpack_masks(words) * valid[:, None, None]).astype(jnp.bfloat16)


def second_half(tiles, item_factors, items):
    return jnp.einsum(
        "siu,sdi->sdu", tiles, item_factors[items], preferred_element_type=jnp.float32
    )


def own_slots(partial_value, row_dir, item_factors, users, items, words, limit):
    group = group_size()
    trips = (limit + group - 1) // group

    def turn(index, acc):
        start = index * group
        part_users = lax.dynamic_slice_in_dim(users, start, group)
        part_items = lax.dynamic_slice_in_dim(items, start, group)
        part_words = lax.dynamic_slice_in_dim(words, start, group)
        valid = (start + jnp.arange(group, dtype=jnp.int32) < limit).astype(jnp.float32)
        tiles = masked_tiles(row_dir, item_factors, part_users, part_items, part_words, valid)
        return acc.at[part_users].add(second_half(tiles, item_factors, part_items))

    return lax.fori_loop(0, trips, turn, partial_value)


def graph_terms(partial_value, row_dir, self_tiles, next_tiles, first_local):
    row_blocks = row_dir.shape[0]
    local = first_local + jnp.arange(self_tiles.shape[0], dtype=jnp.int32)
    after = jnp.minimum(local + 1, row_blocks - 1)
    keep = (local < row_blocks - 1).astype(jnp.int32)
    own = row_dir[local]
    following = row_dir[after]
    sym_weights = self_tiles + jnp.swapaxes(self_tiles, 1, 2)
    edge_weights = next_tiles * keep[:, None, None]
    degree = jnp.sum(sym_weights, axis=2).astype(jnp.float32) + jnp.sum(
        edge_weights, axis=2
    ).astype(jnp.float32)
    column_degree = jnp.sum(edge_weights, axis=1).astype(jnp.float32)
    sym = sym_weights.astype(jnp.bfloat16)
    edges = edge_weights.astype(jnp.bfloat16)
    here = degree[:, None, :] * own.astype(jnp.float32) - jnp.einsum(
        "buv,bdv->bdu", sym, own, preferred_element_type=jnp.float32
    )
    here = here - jnp.einsum("buv,bdv->bdu", edges, following, preferred_element_type=jnp.float32)
    there = column_degree[:, None, :] * following.astype(jnp.float32) - jnp.einsum(
        "buv,bdu->bdv", edges, own, preferred_element_type=jnp.float32
    )
    partial_value = partial_value.at[local].add(graph_weight * here)
    return partial_value.at[after].add(graph_weight * there)


def per_device(
    rhs, item_factors, slot_users, slot_items, slot_counts, mask_words, self_tiles, next_tiles
):
    users = slot_users[0, 0]
    items = slot_items[0, 0]
    words = mask_words[0, 0]
    count = slot_counts[0, 0]
    count_dev = self_tiles.shape[0]
    first_local = lax.axis_index(COL) * count_dev
    solution = jnp.zeros_like(rhs)
    residual = rhs
    direction = rhs
    mine = residual
    norm_now = one_axis_at_a_time(jnp.sum(mine * mine), ROW_COL)
    for iteration in range(ITERS):
        apply_row_dir = gathered_copies(direction.astype(jnp.bfloat16), COL, 0)
        partial_value = jnp.zeros(apply_row_dir.shape, jnp.float32)
        partial_value = own_slots(
            partial_value, apply_row_dir, item_factors, users, items, words, count
        )
        apply_partial_value = graph_terms(
            partial_value, apply_row_dir, self_tiles, next_tiles, first_local
        )
        image = sum_at_owner(apply_partial_value, COL, 0) + ridge_weight * direction
        curve, cross, square = (
            one_axis_at_a_time(jnp.sum(direction * image), ROW_COL),
            one_axis_at_a_time(jnp.sum(residual * image), ROW_COL),
            one_axis_at_a_time(jnp.sum(image * image), ROW_COL),
        )
        alpha = norm_now / curve
        solution = solution + alpha * direction
        residual = residual - alpha * image
        norm_next = norm_now - 2.0 * alpha * cross + alpha * alpha * square
        direction = residual + norm_next / norm_now * direction
        norm_now = norm_next
    return (solution, residual)


def solution(mesh):
    finer = Mesh(mesh.devices.reshape(8, 4, 8, 2), ("row_0", "row_1", "col_0", "col_1"))
    return jax.shard_map(
        per_device,
        mesh=finer,
        in_specs=(
            P(ROW_COL, None, None),
            P(COL, None, None),
            P(ROW, COL, None),
            P(ROW, COL, None),
            P(ROW, COL),
            P(ROW, COL, None, None, None),
            P(ROW_COL, None, None),
            P(ROW_COL, None, None),
        ),
        out_specs=(P(ROW_COL, None, None), P(ROW_COL, None, None)),
        check_vma=False,
    )
```

profile of v0, /device:TPU:1, one launch (start us, length us, event | category | flops | bytes accessed | tf_op | source)
XLA Modules:
  0.0 243.7 jit_solution(6301255121882142461)
XLA Ops:
  0.6 0.9 convert_bitcast_fusion.1
  1.5 0.7 broadcast_in_dim.28
  2.2 10.2 %all-to-all-start = ((bf16[16,1,64,128]{3,2,1,0:T(8,128)(2,1)}), bf16[16,1,64,128]{3,2,1,0:T(8,128)(2,1)S(1)}, u32[]{:S(2)}, u32[]{:S(2)}) async-start(bf16[16,1,64,128]{3,2,1,0:T(8,128)(2,1)} %broadcast_in_dim.28), calls=%async_computation | async-start | bytes 524288 | tf_op jit(solution)/shard_map/all_to_all | solution.py:25
  13.2 1.0 multiply_reduce_fusion
  14.2 0.6 copy-done.5
  14.8 0.8 and_reduce_fusion
  15.6 8.5 %all-to-all-done = bf16[16,1,64,128]{3,2,1,0:T(8,128)(2,1)S(1)} async-done(((bf16[16,1,64,128]{3,2,1,0:T(8,128)(2,1)}), bf16[16,1,64,128]{3,2,1,0:T(8,128)(2,1)S(1)}, u32[]{:S(2)}, u32[]{:S(2)}) %all-to-all-start) | async-done | bytes 262176 | tf_op jit(solution)/shard_map/all_to_all | solution.py:25
  24.8 9.8 %while.28 = (s32[]{:T(128)}, f32[16,64,128]{2,1,0:T(8,128)S(1)}, s32[]{:T(128)}, s32[96]{0:T(128)S(1)}, s32[96]{0:T(128)S(1)}, /*index=5*/bf16[64,64,128]{2,1,0:...) while((s32[]{:T(128)}, f32[16,64,128]{2,1,0:T(8,128)S(1)}, ...), condition=%wide.region_7.8_spmd, body=%wide.region_5.7_spmd.sunk | while | flops 68815000 | bytes 4074363 | solution.py:86
  24.8 0.6 compare_convert_fusion.4
  25.7 0.9 constant_dynamic-slice_fusion.4
  27.2 0.6 gather_fusion
  28.4 1.3 scatter_fusion
  29.7 0.7 compare_convert_fusion.4
  30.6 0.9 constant_dynamic-slice_fusion.4
  31.5 0.6 gather_fusion.1
  33.3 1.3 scatter_fusion
  34.8 0.8 fusion.32
  35.7 0.7 fusion.36
  36.4 38.9 %all_to_all.20 = f32[16,1,64,128]{3,2,1,0:T(8,128)S(1)} all-to-all(f32[16,1,64,128]{3,2,1,0:T(8,128)S(1)} %bitcast.177), channel_id=1, replica_groups=mesh['row_0'=8,'row_1'=4,'col_0'=8,'col_1'=2] {'col_0','col_1'}, dimensions={0} | all-to-all | bytes 1048576 | tf_op jit(solution)/shard_map/all_to_all | solution.py:40
  75.4 0.7 copy-done.1
  76.1 0.7 multiply_reduce_fusion.3
  76.8 19.1 %all-reduce.1 = (f32[]{:T(128)}, f32[]{:T(128)}, f32[]{:T(128)}) all-reduce(f32[]{:T(128)} %get-tuple-element.196, f32[]{:T(128)} %get-tuple-element.193, f32[]{:T(128)} %get-tuple-element.192), channel_id=1, replica_groups=mesh['row_0'=8,'row_1'=4,'col_0'=8,'col_1'=2] {'row_0'}, use_global_device_ids=true, to_apply=%region_1.0 | all-reduce | flops 3 | bytes 24 | tf_op jit(solution)/shard_map/psum | solution.py:46
  95.9 9.4 %all-reduce.2 = (f32[]{:T(128)}, f32[]{:T(128)}, f32[]{:T(128)}) all-reduce(f32[]{:T(128)} %get-tuple-element.238, f32[]{:T(128)} %get-tuple-element.239, f32[]{:T(128)} %get-tuple-element.240), channel_id=1, replica_groups=mesh['row_0'=8,'row_1'=4,'col_0'=8,'col_1'=2] {'row_1'}, use_global_device_ids=true, to_apply=%region_2.0 | all-reduce | flops 3 | bytes 24 | tf_op jit(solution)/shard_map/psum | solution.py:46
  105.2 11.4 %all-reduce = (f32[]{:T(128)}, f32[]{:T(128)}, f32[]{:T(128)}) all-reduce(f32[]{:T(128)} %get-tuple-element.241, f32[]{:T(128)} %get-tuple-element.242, f32[]{:T(128)} %get-tuple-element.243), channel_id=1, replica_groups=mesh['row_0'=8,'row_1'=4,'col_0'=8,'col_1'=2] {'col_0'}, use_global_device_ids=true, to_apply=%region_3.0 | all-reduce | flops 3 | bytes 24 | tf_op jit(solution)/shard_map/psum | solution.py:46
  116.6 11.3 %all-reduce.3 = (f32[]{:T(128)}, f32[]{:T(128)}, f32[]{:T(128)}) all-reduce(f32[]{:T(128)} %get-tuple-element.235, f32[]{:T(128)} %get-tuple-element.236, f32[]{:T(128)} %get-tuple-element.237), channel_id=1, replica_groups=mesh['row_0'=8,'row_1'=4,'col_0'=8,'col_1'=2] {'col_1'}, use_global_device_ids=true, to_apply=%region_4.0 | all-reduce | flops 3 | bytes 24 | tf_op jit(solution)/shard_map/psum | solution.py:46
  131.8 0.7 broadcast_in_dim.32
  132.6 6.3 %all-to-all-start.2 = ((bf16[16,1,64,128]{3,2,1,0:T(8,128)(2,1)}), bf16[16,1,64,128]{3,2,1,0:T(8,128)(2,1)S(1)}, u32[]{:S(2)}, u32[]{:S(2)}) async-start(bf16[16,1,64,128]{3,2,1,0:T(8,128)(2,1)} %broadcast_in_dim.32), calls=%async_computation.2 | async-start | bytes 524288 | tf_op jit(solution)/shard_map/all_to_all | solution.py:25
  138.9 11.6 %all-to-all-done.2 = bf16[16,1,64,128]{3,2,1,0:T(8,128)(2,1)S(1)} async-done(((bf16[16,1,64,128]{3,2,1,0:T(8,128)(2,1)}), bf16[16,1,64,128]{3,2,1,0:T(8,128)(2,1)S(1)}, u32[]{:S(2)}, u32[]{:S(2)}) %all-to-all-start.2) | async-done | bytes 262176 | tf_op jit(solution)/shard_map/all_to_all | solution.py:25
  150.5 9.8 %while.29 = (s32[]{:T(128)}, f32[16,64,128]{2,1,0:T(8,128)S(1)}, s32[]{:T(128)}, s32[96]{0:T(128)S(1)}, s32[96]{0:T(128)S(1)}, /*index=5*/bf16[64,64,128]{2,1,0:...) while((s32[]{:T(128)}, f32[16,64,128]{2,1,0:T(8,128)S(1)}, ...), condition=%wide.region_26.27_spmd, body=%wide.region_24.26_spmd.sunk | while | flops 68815000 | bytes 4074363 | solution.py:86
  150.6 0.7 compare_convert_fusion.5
  151.4 0.9 constant_dynamic-slice_fusion.5
  152.3 0.6 gather_fusion.3
  153.0 0.6 gather_fusion.2
  154.1 1.3 scatter_fusion.1
  155.5 0.7 compare_convert_fusion.5
  156.3 0.9 constant_dynamic-slice_fusion.5
  157.3 0.6 gather_fusion.3
  157.9 0.6 gather_fusion.2
  159.0 1.3 scatter_fusion.1
  160.5 0.8 fusion.39
  161.4 0.7 fusion.43
  162.1 39.1 %all_to_all.21 = f32[16,1,64,128]{3,2,1,0:T(8,128)S(1)} all-to-all(f32[16,1,64,128]{3,2,1,0:T(8,128)S(1)} %bitcast.176), channel_id=1, replica_groups=mesh['row_0'=8,'row_1'=4,'col_0'=8,'col_1'=2] {'col_0','col_1'}, dimensions={0} | all-to-all | bytes 1048576 | tf_op jit(solution)/shard_map/all_to_all | solution.py:40
  201.3 0.6 multiply_reduce_fusion.2
  201.9 11.6 %psum.136 = f32[]{:T(128)} all-reduce(f32[]{:T(128)} %multiply_reduce_fusion.2), channel_id=1, replica_groups=mesh['row_0'=8,'row_1'=4,'col_0'=8,'col_1'=2] {'row_0'}, use_global_device_ids=true, to_apply=%region_29.30 | all-reduce | flops 1 | bytes 8 | tf_op jit(solution)/shard_map/psum | solution.py:46
  213.5 6.6 %psum.137 = f32[]{:T(128)} all-reduce(f32[]{:T(128)} %psum.136), channel_id=1, replica_groups=mesh['row_0'=8,'row_1'=4,'col_0'=8,'col_1'=2] {'row_1'}, use_global_device_ids=true, to_apply=%region_30.31 | all-reduce | flops 1 | bytes 8 | tf_op jit(solution)/shard_map/psum | solution.py:46
  220.1 11.3 %psum.138 = f32[]{:T(128)} all-reduce(f32[]{:T(128)} %psum.137), channel_id=1, replica_groups=mesh['row_0'=8,'row_1'=4,'col_0'=8,'col_1'=2] {'col_0'}, use_global_device_ids=true, to_apply=%region_31.32 | all-reduce | flops 1 | bytes 8 | tf_op jit(solution)/shard_map/psum | solution.py:46
  231.4 11.0 %psum.139 = f32[]{:T(128)} all-reduce(f32[]{:T(128)} %psum.138), channel_id=1, replica_groups=mesh['row_0'=8,'row_1'=4,'col_0'=8,'col_1'=2] {'col_1'}, use_global_device_ids=true, to_apply=%region_32.33 | all-reduce | flops 1 | bytes 8 | tf_op jit(solution)/shard_map/psum | solution.py:46
  243.0 0.6 multiply_subtract_fusion
  (48 shorter events, 5.5 us)
Async XLA Ops:
  0.6 12.4 %copy-start.2 = (s32[1,128,128]{2,1,0:T(8,128)S(1)}, s32[1,128,128]{2,1,0:T(8,128)}, u32[]{:S(2)}) copy-start(s32[1,128,128]{2,1,0:T(8,128)} %param.26) | copy-start | bytes 196612
  0.6 23.6 %copy-start = (bf16[64,64,128]{2,1,0:T(8,128)(2,1)S(1)}, bf16[64,64,128]{2,1,0:T(8,128)(2,1)}, u32[]{:S(2)}) copy-start(bf16[64,64,128]{2,1,0:T(8,128)(2,1)} %param.21) | copy-start | bytes 3145732
  2.2 21.9 %all-to-all-start = ((bf16[16,1,64,128]{3,2,1,0:T(8,128)(2,1)}), bf16[16,1,64,128]{3,2,1,0:T(8,128)(2,1)S(1)}, u32[]{:S(2)}, u32[]{:S(2)}) async-start(bf16[16,1,64,128]{3,2,1,0:T(8,128)(2,1)} %broadcast_in_dim.28), calls=%async_computation | async-start | bytes 524288 | tf_op jit(solution)/shard_map/all_to_all | solution.py:25
  14.2 0.7 copy-start.5
  24.2 0.7 copy-start.3
  24.2 0.7 copy-start.4
  75.3 0.8 copy-start.1
  132.6 17.9 %all-to-all-start.2 = ((bf16[16,1,64,128]{3,2,1,0:T(8,128)(2,1)}), bf16[16,1,64,128]{3,2,1,0:T(8,128)(2,1)S(1)}, u32[]{:S(2)}, u32[]{:S(2)}) async-start(bf16[16,1,64,128]{3,2,1,0:T(8,128)(2,1)} %broadcast_in_dim.32), calls=%async_computation.2 | async-start | bytes 524288 | tf_op jit(solution)/shard_map/all_to_all | solution.py:25
where the time goes:
time: 245 us; the launch traced here: 244 us
  blocking collectives  170 us (69%)
  waiting for transfers between devices  20.1 us (8%)
  starting transfers between devices  16.5 us (7%)
  other arithmetic  13 us (5%)
  local copies, waits for them, and re-layouts  12.6 us (5%)
  between operations  6.04 us (2%)
  matrix products  5.56 us (2%)
    psum x8, blocking collectives, one_axis_at_a_time(): x = lax.psum(x, axis)  91.6 us
    all_to_all x2, blocking collectives, sum_at_owner(): blocks = lax.all_to_all(split_up(x, dim, size), axis, 0, 0, tiled=True)  78.1 us
    all_to_all x2, waiting for transfers between devices, from_everyone(): lax.all_to_all(jnp.broadcast_to(x[None], (size, *x.shape)), axis, 0, 0, t...  20.1 us
    all_to_all x2, starting transfers between devices, from_everyone(): lax.all_to_all(jnp.broadcast_to(x[None], (size, *x.shape)), axis, 0, 0, t...  16.5 us
    scatter-add x4, other arithmetic, turn(): return acc.at[part_users].add(second_half(tiles, item_factors, part_items))  5.36 us
  transfers between devices with their start and end apart: 2, of which 2 were waited for; matrix products, arithmetic and copies ran while one was open for 1% of the time, Pallas kernels for 0%

commit v1 on v0

v1 whole, which is shorter than its diff:
```python
import functools

import jax
import jax.numpy as jnp
from jax import lax
from jax.experimental import pallas as pl
from jax.experimental.pallas import tpu as pltpu
from jax.sharding import PartitionSpec as P

GRAPH = 0.01
RIDGE = 0.5
UNROLL = 8
f32, bf16, i32 = jnp.float32, jnp.bfloat16, jnp.int32


def far_first(cols):
    chips = cols // 2
    order = sorted(range(1, chips), key=lambda o: -min(o, chips - o))
    return order


def kernel(
    rows,
    cols,
    rhs_ref,
    items_hbm,
    users_ref,
    slot_items_ref,
    count_ref,
    words_hbm,
    self_hbm,
    next_hbm,
    sol_ref,
    res_ref,
    a_ref,
    at_ref,
    w_ref,
    m_ref,
    t_ref,
    s_ref,
    r1_ref,
    r2_ref,
    x1_ref,
    x2_ref,
    y1_ref,
    y2_ref,
    self_ref,
    next_ref,
    sym_ref,
    e_ref,
    et_ref,
    code_ref,
    code_sm,
    p1_ref,
    p2_ref,
    p3_ref,
    local_sem,
    g1_send,
    g1_recv,
    x1_send,
    x1_recv,
    p1_send,
    p1_recv,
    g2_send,
    g2_recv,
    x2_send,
    x2_recv,
    p2_send,
    p2_recv,
    p3_send,
    p3_recv,
):
    slots = w_ref.shape[0]
    blocks = a_ref.shape[0]
    me = lax.axis_index("col")
    my_row = lax.axis_index("row")
    my_chip, my_core = me // 2, me % 2
    chips = cols // 2

    def peers():
        for o in far_first(cols):
            chip = lax.rem(my_chip + o, chips)
            for c in (0, 1):
                yield 2 * o + c - 2, chip * 2 + lax.rem(my_core + c, 2)
        yield 2 * chips - 2, my_chip * 2 + 1 - my_core

    loads = [
        pltpu.make_async_copy(self_hbm.at[0], self_ref, local_sem.at[0]),
        pltpu.make_async_copy(next_hbm.at[0], next_ref, local_sem.at[1]),
        pltpu.make_async_copy(items_hbm, a_ref, local_sem.at[2]),
        pltpu.make_async_copy(words_hbm.at[0, 0], w_ref, local_sem.at[3]),
    ]
    for load in loads:
        load.start()

    barrier = pltpu.get_barrier_semaphore()
    for _, peer in peers():
        pl.semaphore_signal(
            barrier, inc=1, device_id={"col": peer}, device_id_type=pl.DeviceIdType.MESH
        )
    for o in range(1, rows):
        pl.semaphore_signal(
            barrier,
            inc=1,
            device_id={"row": lax.rem(my_row + o, rows)},
            device_id_type=pl.DeviceIdType.MESH,
        )

    rhs = rhs_ref[0]
    r1_ref[pl.ds(me, 1)] = rhs.astype(bf16)[None]
    r1_ref[cols] = jnp.zeros(r1_ref.shape[1:], bf16)
    r2_ref[cols] = jnp.zeros(r2_ref.shape[1:], bf16)
    s_ref[0] = jnp.zeros(s_ref.shape[1:], f32)

    lane = lax.broadcasted_iota(i32, (1, 128), 1)
    code_ref[...] = jnp.broadcast_to((cols + 1) * 8192 + lane * 64, (8, 128))
    slot = lax.broadcasted_iota(i32, (1, slots), 1)
    user = jnp.where(slot < count_ref[0, 0], users_ref[0], cols)
    code_ref[0:1, 0:slots] = user * 8192 + slot * 64 + slot_items_ref[0]
    across = jnp.broadcast_to(code_ref[0:1, :].astype(f32), (128, 128))
    down = across.T
    rank = jnp.sum(jnp.where(across < down, 1.0, 0.0), axis=1, keepdims=True)
    lanes = lax.broadcasted_iota(i32, (128, 128), 1).astype(f32)
    ordered = jnp.sum(jnp.where(rank == lanes, down, 0.0), axis=0, keepdims=True)
    upto = jnp.sum(jnp.where(down < (lanes + 1.0) * 8192.0, 1.0, 0.0), axis=0, keepdims=True)
    before = jnp.sum(jnp.where(down < lanes * 8192.0, 1.0, 0.0), axis=0, keepdims=True)
    code_ref[0:1, :] = ordered.astype(i32)
    code_ref[1:2, :] = jnp.where(upto > before, upto, 0.0).astype(i32)
    to_scalars = pltpu.make_async_copy(code_ref, code_sm, local_sem.at[4])
    to_scalars.start()

    pl.semaphore_wait(barrier, cols - 1 + rows - 1)

    def gather(r_ref, send, recv):
        return [
            pltpu.make_async_remote_copy(
                src_ref=r_ref.at[me],
                dst_ref=r_ref.at[me],
                send_sem=send.at[i],
                recv_sem=recv.at[me],
                device_id={"col": peer},
                device_id_type=pl.DeviceIdType.MESH,
            )
            for i, peer in peers()
        ]

    def arrive(ref, recv):
        for i, peer in peers():
            pltpu.make_async_copy(ref.at[peer], ref.at[peer], recv.at[peer]).wait()

    sent1 = gather(r1_ref, g1_send, g1_recv)
    for copy in sent1:
        copy.start()

    loads[0].wait()
    loads[1].wait()
    first = self_ref[...].astype(f32)
    sym = first + first.T
    keep = jnp.where(me < cols - 1, 1.0, 0.0)
    edges = next_ref[...].astype(f32) * keep
    edges_t = edges.T
    there_degree = jnp.sum(edges, axis=0, keepdims=True)
    here_degree = jnp.sum(sym, axis=0, keepdims=True) + jnp.sum(edges_t, axis=0, keepdims=True)
    sym_ref[...] = sym.astype(bf16)
    e_ref[...] = edges.astype(bf16)
    et_ref[...] = edges_t.astype(bf16)
    after = jnp.minimum(me + 1, cols - 1)

    loads[2].wait()

    def turn_block(b, carry):
        at_ref[b] = a_ref[b].astype(f32).T.astype(bf16)
        return carry

    lax.fori_loop(0, blocks, turn_block, 0, unroll=4)
    loads[3].wait()
    bit = jnp.left_shift(1, lax.broadcasted_iota(i32, (8, 128), 0))

    def open_mask(s, carry):
        for pair in range(8):
            parts = []
            for w in (2 * pair, 2 * pair + 1):
                word = jnp.broadcast_to(w_ref[s, w : w + 1, :], (8, 128))
                parts.append(jnp.where((word & bit) != 0, 1.0, 0.0))
            m_ref[s, 16 * pair : 16 * pair + 16, :] = jnp.concatenate(parts, axis=0).astype(bf16)
        return carry

    lax.fori_loop(0, slots, open_mask, 0, unroll=2)
    to_scalars.wait()

    def product(r_ref):
        def first_half(k, carry):
            code = code_sm[0, k]
            item = jnp.minimum(code & 63, blocks - 1)
            s, u = jnp.minimum((code >> 6) & 127, slots - 1), jnp.minimum((code >> 13) & 31, cols)
            scores = jnp.dot(at_ref[item], r_ref[u], preferred_element_type=f32)
            t_ref[k] = scores.astype(bf16) * m_ref[s]
            return carry

        def second_half(k, carry):
            acc, last = carry
            code = code_sm[0, k]
            item, u = jnp.minimum(code & 63, blocks - 1), code >> 13
            part = jnp.dot(a_ref[item], t_ref[k], preferred_element_type=f32)
            acc = jnp.where(u == last, acc, 0.0) + part
            s_ref[k + 1] = acc
            return acc, u

        lax.fori_loop(0, slots, first_half, 0, unroll=UNROLL)
        lax.fori_loop(
            0, slots, second_half, (jnp.zeros(s_ref.shape[1:], f32), i32(-1)), unroll=UNROLL
        )

    def summed(u):
        return s_ref[jnp.minimum(code_sm[1, u] & 127, slots)]

    def graph(r_ref):
        own, following = r_ref[me], r_ref[after]
        here = here_degree * own.astype(f32)
        here = here - jnp.dot(own, sym_ref[...], preferred_element_type=f32)
        here = here - jnp.dot(following, et_ref[...], preferred_element_type=f32)
        there = there_degree * following.astype(f32)
        there = there - jnp.dot(own, e_ref[...], preferred_element_type=f32)
        return GRAPH * here, GRAPH * there

    def partial(r_ref, x_ref, y_ref, send, recv):
        here, there = graph(r_ref)
        form = jnp.zeros(here.shape, f32)
        copies = []
        for i, peer in peers():
            value = summed(peer) + jnp.where(peer == me + 1, there, 0.0)
            form = form + r_ref[peer].astype(f32) * value
            x_ref[pl.ds(peer, 1)] = value.astype(bf16)[None]
            copy = pltpu.make_async_remote_copy(
                src_ref=x_ref.at[peer],
                dst_ref=y_ref.at[me],
                send_sem=send.at[i],
                recv_sem=recv.at[me],
                device_id={"col": peer},
                device_id_type=pl.DeviceIdType.MESH,
            )
            copy.start()
            copies.append(copy)
        own = summed(me) + here
        form = form + r_ref[me].astype(f32) * own
        return own, form, copies

    def total(own, y_ref, recv):
        for i, peer in peers():
            pltpu.make_async_copy(y_ref.at[peer], y_ref.at[peer], recv.at[peer]).wait()
            own = own + y_ref[peer].astype(f32)
        return own

    def by_lane(x):
        return jnp.sum(x, axis=0, keepdims=True)

    sublane = lax.broadcasted_iota(i32, (8, 128), 0)

    def stack(*lines):
        out = jnp.zeros((8, 128), f32)
        for n, line in enumerate(lines):
            out = jnp.where(sublane == n, line, out)
        return out

    def share(p_ref, value, send, recv):
        p_ref[pl.ds(me, 1)] = value[None]
        copies = gather(p_ref, send, recv)
        for copy in copies:
            copy.start()
        return copies

    def over_lanes(x):
        return jnp.sum(x, axis=1, keepdims=True)

    arrive(r1_ref, g1_recv)
    product(r1_ref)
    own, form, sent2 = partial(r1_ref, x1_ref, y1_ref, x1_send, x1_recv)
    form = form + RIDGE * rhs * rhs
    sent3 = share(p1_ref, stack(by_lane(rhs * rhs), by_lane(form)), p1_send, p1_recv)
    arrive(p1_ref, p1_recv)
    line = jnp.sum(p1_ref[...], axis=0)
    norm_line, form_line = line[0:1, :], line[1:2, :]
    norm_row, form_row = over_lanes(norm_line), over_lanes(form_line)
    shift = jnp.where(norm_row > 0.0, form_row / jnp.where(norm_row > 0.0, norm_row, 1.0), 0.0)
    w = total(own, y1_ref, x1_recv) + RIDGE * rhs

    v = w - shift * rhs
    r2_ref[pl.ds(me, 1)] = v.astype(bf16)[None]
    sent4 = gather(r2_ref, g2_send, g2_recv)
    for copy in sent4:
        copy.start()
    square = by_lane(w * w)
    arrive(r2_ref, g2_recv)
    product(r2_ref)
    own, form, sent5 = partial(r2_ref, x2_ref, y2_ref, x2_send, x2_recv)
    form = form + RIDGE * v * v
    sent6 = share(p2_ref, stack(square, by_lane(form)), p2_send, p2_recv)
    arrive(p2_ref, p2_recv)
    line = jnp.sum(p2_ref[...], axis=0)
    square_line, bent_line = line[0:1, :], line[1:2, :]
    cubic_line = bent_line + 2.0 * shift * square_line - shift * shift * form_line
    p3_ref[pl.ds(my_row, 1)] = stack(norm_line, form_line, square_line, cubic_line)[None]
    sent7 = []
    for o in range(1, rows):
        copy = pltpu.make_async_remote_copy(
            src_ref=p3_ref.at[my_row],
            dst_ref=p3_ref.at[my_row],
            send_sem=p3_send.at[o - 1],
            recv_sem=p3_recv.at[my_row],
            device_id={"row": lax.rem(my_row + o, rows)},
            device_id_type=pl.DeviceIdType.MESH,
        )
        copy.start()
        sent7.append(copy)
    hv = total(own, y2_ref, x2_recv) + RIDGE * v
    z = hv + shift * w
    for o in range(1, rows):
        other = lax.rem(my_row + o, rows)
        pltpu.make_async_copy(p3_ref.at[other], p3_ref.at[other], p3_recv.at[other]).wait()
    sums = over_lanes(jnp.sum(p3_ref[...], axis=0))
    norm0, form1, square1, cubic1 = (sums[n : n + 1, :] for n in range(4))
    alpha1 = norm0 / form1
    norm1 = norm0 - 2.0 * alpha1 * form1 + alpha1 * alpha1 * square1
    more = 1.0 + norm1 / norm0
    curve = more * more * form1 - 2.0 * more * alpha1 * square1 + alpha1 * alpha1 * cubic1
    alpha2 = norm1 / curve
    direction = more * rhs - alpha1 * w
    image = more * w - alpha1 * z
    sol_ref[0] = alpha1 * rhs + alpha2 * direction
    res_ref[0] = rhs - alpha1 * w - alpha2 * image

    for copies in (sent1, sent2, sent3, sent4, sent5, sent6, sent7):
        for copy in copies:
            copy.wait_send()


def per_device(rows, cols, *args):
    rhs, items, users, slot_items, counts, words, selfs, nexts = args
    slots = users.shape[2]
    blocks, rank, width = items.shape
    vmem = pl.BlockSpec(memory_space=pltpu.VMEM)
    smem = pl.BlockSpec(memory_space=pltpu.SMEM)
    hbm = pl.BlockSpec(memory_space=pl.ANY)
    dma = pltpu.SemaphoreType.DMA
    pair = [dma((cols - 1,)), dma((cols,))]
    block16 = (cols, rank, width)
    return pl.pallas_call(
        functools.partial(kernel, rows, cols),
        out_shape=[jax.ShapeDtypeStruct(rhs.shape, f32)] * 2,
        in_specs=[vmem, hbm, vmem, vmem, smem, hbm, hbm, hbm],
        out_specs=[vmem, vmem],
        scratch_shapes=[
            pltpu.VMEM((blocks, rank, width), bf16),
            pltpu.VMEM((blocks, width, rank), bf16),
            pltpu.VMEM((slots, width // 8, width), i32),
            pltpu.VMEM((slots, width, width), bf16),
            pltpu.VMEM((slots, width, width), bf16),
            pltpu.VMEM((slots + 1, rank, width), f32),
            pltpu.VMEM((cols + 1, rank, width), bf16),
            pltpu.VMEM((cols + 1, rank, width), bf16),
            pltpu.VMEM(block16, bf16),
            pltpu.VMEM(block16, bf16),
            pltpu.VMEM(block16, bf16),
            pltpu.VMEM(block16, bf16),
            pltpu.VMEM((width, width), i32),
            pltpu.VMEM((width, width), i32),
            pltpu.VMEM((width, width), bf16),
            pltpu.VMEM((width, width), bf16),
            pltpu.VMEM((width, width), bf16),
            pltpu.VMEM((8, 128), i32),
            pltpu.SMEM((8, 128), i32),
            pltpu.VMEM((cols, 8, 128), f32),
            pltpu.VMEM((cols, 8, 128), f32),
            pltpu.VMEM((rows, 8, 128), f32),
            dma((5,)),
            *pair * 6,
            dma((rows - 1,)),
            dma((rows,)),
        ],
        compiler_params=pltpu.CompilerParams(collective_id=0, has_side_effects=True),
        name="cg",
    )(*args)


def solution(mesh):
    rows, cols = mesh.shape["row"], mesh.shape["col"]
    user_blocks = P(("row", "col"), None, None)
    return jax.shard_map(
        functools.partial(per_device, rows, cols),
        mesh=mesh,
        in_specs=(
            user_blocks,
            P("col", None, None),
            P("row", "col", None),
            P("row", "col", None),
            P("row", "col"),
            P("row", "col", None, None, None),
            user_blocks,
            user_blocks,
        ),
        out_specs=(user_blocks, user_blocks),
        check_vma=False,
    )
```

time: 245 us -> 76.3 us (0.31)
  blocking collectives: 170 us -> 0 us
  Pallas kernels: 0 us -> 72.7 us
  waiting for transfers between devices: 20.1 us -> 0 us
  starting transfers between devices: 16.5 us -> 0 us
  other arithmetic: 13 us -> 0 us
  local copies, waits for them, and re-layouts: 12.6 us -> 2 us
  matrix products: 5.56 us -> 0 us
  between operations: 6.04 us -> 1.29 us
    psum x8 -> x0, blocking collectives: 91.6 us -> none  [one_axis_at_a_time(): x = lax.psum(x, axis)]
    all_to_all x2 -> x0, blocking collectives: 78.1 us -> none  [sum_at_owner(): blocks = lax.all_to_all(split_up(x, dim, size), axis, 0, 0, tiled=True)]
    pallas_call x0 -> x1, Pallas kernels: none -> 72.7 us  [per_device(): pl.pallas_call(functools.partial(kernel, rows, cols), out_shape=[jax.Shap...]
    all_to_all x2 -> x0, waiting for transfers between devices: 20.1 us -> none  [from_everyone(): lax.all_to_all(jnp.broadcast_to(x[None], (size, *x.shape)), axis, 0, 0, t...]
    all_to_all x2 -> x0, starting transfers between devices: 16.5 us -> none  [from_everyone(): lax.all_to_all(jnp.broadcast_to(x[None], (size, *x.shape)), axis, 0, 0, t...]
    dot_general x10 -> x0, matrix products: 5.56 us -> none  [the longest x4 2.26 us: second_half(): jnp.einsum('siu,sdi->sdu', tiles, item_factors[items], preferred_element_...]
    scatter-add x4 -> x0, other arithmetic: 5.36 us -> none  [turn(): return acc.at[part_users].add(second_half(tiles, item_factors, part_items))]
    gather x8 -> x0, local copies, waits for them, and re-layouts: 4.78 us -> none  [the longest x4 2.39 us: masked_tiles(): row_dir[users]]
  transfers between devices with their start and end apart: 2 -> 0, of which waited for: 2 -> 0; matrix products, arithmetic and copies ran while one was open for 1% -> 0% of each run, Pallas kernels for 0% -> 0%
where the time goes in v1:
time: 76.3 us; the launch traced here: 76 us
  Pallas kernels  72.7 us (95%)
  local copies, waits for them, and re-layouts  2 us (3%)
  between operations  1.29 us (2%)
    pallas_call x1, Pallas kernels, per_device(): pl.pallas_call(functools.partial(kernel, rows, cols), out_shape=[jax.Shap...  72.7 us
    unnamed x4, local copies, waits for them, and re-layouts  2 us

profile of v1, /device:TPU:1, one launch (start us, length us, event | category | flops | bytes accessed | tf_op | source)
XLA Modules:
  0.0 76.0 jit_solution(16141251882649710689)
XLA Ops:
  1.3 72.7 %cg.1 = (f32[1,64,128]{2,1,0:T(8,128)}, f32[1,64,128]{2,1,0:T(8,128)}) custom-call(f32[1,64,128]{2,1,0:T(8,128)} %rhs_ref.1, bf16[64,64,128]{2,1,0:T(8,128)(2,1)} %items_hbm.1, s32[1,1,96]{2,1,0:T(1,128)} %users_ref.1, s32[1,1,96]{2,1,0:T(1,128)} %slot_items_ref.1, s32[1,1]{1,0:T(1,128)S(6)} %copy.12.count_ref, s32[1,1,96,16,128]{4,3,2,1,0:T(8,128)} %words_hbm.1, ...), custom_call_target="tpu_custom_call" | custom-call | tf_op jit(solution)/shard_map/cg/pallas_call | solution.py:347
  74.0 0.0 copy-start
  74.0 1.4 %copy.13 = f32[1,64,128]{2,1,0:T(8,128)} copy(f32[1,64,128]{2,1,0:T(8,128)} %get-tuple-element.4) | data formatting | bytes 65536
  75.4 0.0 copy-done
  75.4 0.6 copy.14
Async XLA Ops:
  74.0 1.4 %copy-start = (f32[1,64,128]{2,1,0:T(8,128)S(1)}, f32[1,64,128]{2,1,0:T(8,128)}, u32[]{:S(2)}) copy-start(f32[1,64,128]{2,1,0:T(8,128)} %get-tuple-element.5) | copy-start | bytes 98308

commit v2 on v1

v2 whole, which is shorter than its diff:
```python
import functools

import jax
import jax.numpy as jnp
from jax import lax
from jax.experimental import pallas as pl
from jax.experimental.pallas import tpu as pltpu
from jax.sharding import PartitionSpec as P

GRAPH = 0.01
RIDGE = 0.5
UNROLL = 8
f32, bf16, i32 = jnp.float32, jnp.bfloat16, jnp.int32


def far_first(chips):
    return sorted(range(1, chips), key=lambda o: -min(o, chips - o))


def kernel(
    rows,
    cols,
    rhs_hbm,
    items_hbm,
    users_hbm,
    slot_items_hbm,
    count_hbm,
    words_hbm,
    self_hbm,
    next_hbm,
    out_ref,
    rhs_ref,
    users_ref,
    slot_items_ref,
    count_ref,
    a_ref,
    at_ref,
    w_ref,
    m_ref,
    t_ref,
    s_ref,
    r1_ref,
    r2_ref,
    x1_ref,
    x2_ref,
    yp1_ref,
    yp2_ref,
    z1_ref,
    z2_ref,
    y1_ref,
    y2_ref,
    self_ref,
    next_ref,
    sym_ref,
    e_ref,
    et_ref,
    code_ref,
    code_sm,
    p1_ref,
    p2_ref,
    p3_ref,
    local_sem,
    g1_send,
    g1_recv,
    g2_send,
    g2_recv,
    p1_send,
    p1_recv,
    p2_send,
    p2_recv,
    xp1_send,
    xp1_recv,
    xp2_send,
    xp2_recv,
    z1_send,
    z1_recv,
    z2_send,
    z2_recv,
    p3_send,
    p3_recv,
):
    slots = w_ref.shape[0]
    blocks = a_ref.shape[0]
    chips = cols // 2
    me = lax.axis_index("col")
    my_row = lax.axis_index("row")
    my_chip, my_core = me // 2, me % 2
    partner = my_chip * 2 + 1 - my_core
    far = far_first(chips)
    near = far[::-1]

    def chip(o):
        return lax.rem(my_chip + o, chips)

    def remote(src, dst, send, recv, where):
        copy = pltpu.make_async_remote_copy(
            src_ref=src,
            dst_ref=dst,
            send_sem=send,
            recv_sem=recv,
            device_id=where,
            device_id_type=pl.DeviceIdType.MESH,
        )
        copy.start()
        return copy

    def arrived(ref, sem):
        pltpu.make_async_copy(ref, ref, sem).wait()

    rhs_load = pltpu.make_async_copy(rhs_hbm.at[0], rhs_ref, local_sem.at[5])
    rhs_load.start()
    barrier = pltpu.get_barrier_semaphore()
    for o in range(1, rows):
        pl.semaphore_signal(
            barrier,
            inc=1,
            device_id={"row": lax.rem(my_row + o, rows)},
            device_id_type=pl.DeviceIdType.MESH,
        )
    for o in range(1, cols):
        pl.semaphore_signal(
            barrier,
            inc=1,
            device_id={"col": lax.rem(me + o, cols)},
            device_id_type=pl.DeviceIdType.MESH,
        )
    loads = [
        pltpu.make_async_copy(users_hbm.at[0], users_ref, local_sem.at[6]),
        pltpu.make_async_copy(slot_items_hbm.at[0], slot_items_ref, local_sem.at[7]),
        pltpu.make_async_copy(count_hbm, count_ref, local_sem.at[8]),
        pltpu.make_async_copy(self_hbm.at[0], self_ref, local_sem.at[0]),
        pltpu.make_async_copy(next_hbm.at[0], next_ref, local_sem.at[1]),
        pltpu.make_async_copy(items_hbm, a_ref, local_sem.at[2]),
        pltpu.make_async_copy(words_hbm.at[0, 0], w_ref, local_sem.at[3]),
    ]
    for load in loads:
        load.start()

    rhs_load.wait()
    rhs = rhs_ref[...]
    r1_ref[pl.ds(me, 1)] = rhs.astype(bf16)[None]
    r1_ref[cols] = jnp.zeros(r1_ref.shape[1:], bf16)
    r2_ref[cols] = jnp.zeros(r2_ref.shape[1:], bf16)
    s_ref[0] = jnp.zeros(s_ref.shape[1:], f32)

    pl.semaphore_wait(barrier, cols - 1 + rows - 1)

    def gather(r_ref, send, recv):
        copies = [
            remote(r_ref.at[me], r_ref.at[me], send.at[n], recv.at[me], {"col": chip(o) * 2 + my_core})
            for n, o in enumerate(far)
        ]
        n = chips - 1
        copies.append(remote(r_ref.at[me], r_ref.at[me], send.at[n], recv.at[me], {"col": partner}))
        return copies

    def pass_on(n, r_ref, send, recv):
        block = chip(near[n]) * 2 + my_core
        arrived(r_ref.at[block], recv.at[block])
        return remote(
            r_ref.at[block], r_ref.at[block], send.at[chips + n], recv.at[block], {"col": partner}
        )

    def finish(r_ref, recv):
        arrived(r_ref.at[partner], recv.at[partner])
        for o in near:
            block = chip(o) * 2 + 1 - my_core
            arrived(r_ref.at[block], recv.at[block])

    sent = gather(r1_ref, g1_send, g1_recv)

    for load in loads[:3]:
        load.wait()
    lane = lax.broadcasted_iota(i32, (1, 128), 1)
    code_ref[...] = jnp.broadcast_to((cols + 1) * 8192 + lane * 64, (8, 128))
    slot = lax.broadcasted_iota(i32, (1, slots), 1)
    user = jnp.where(slot < count_ref[...], users_ref[...], cols)
    code_ref[0:1, 0:slots] = user * 8192 + slot * 64 + slot_items_ref[...]
    across = jnp.broadcast_to(code_ref[0:1, :].astype(f32), (128, 128))
    down = across.T
    rank = jnp.sum(jnp.where(across < down, 1.0, 0.0), axis=1, keepdims=True)
    lanes = lax.broadcasted_iota(i32, (128, 128), 1).astype(f32)
    ordered = jnp.sum(jnp.where(rank == lanes, down, 0.0), axis=0, keepdims=True)
    upto = jnp.sum(jnp.where(down < (lanes + 1.0) * 8192.0, 1.0, 0.0), axis=0, keepdims=True)
    before = jnp.sum(jnp.where(down < lanes * 8192.0, 1.0, 0.0), axis=0, keepdims=True)
    code_ref[0:1, :] = ordered.astype(i32)
    code_ref[1:2, :] = jnp.where(upto > before, upto, 0.0).astype(i32)
    to_scalars = pltpu.make_async_copy(code_ref, code_sm, local_sem.at[4])
    to_scalars.start()

    loads[3].wait()
    loads[4].wait()
    first = self_ref[...].astype(f32)
    sym = first + first.T
    keep = jnp.where(me < cols - 1, 1.0, 0.0)
    edges = next_ref[...].astype(f32) * keep
    edges_t = edges.T
    there_degree = jnp.sum(edges, axis=0, keepdims=True)
    here_degree = jnp.sum(sym, axis=0, keepdims=True) + jnp.sum(edges_t, axis=0, keepdims=True)
    sym_ref[...] = sym.astype(bf16)
    e_ref[...] = edges.astype(bf16)
    et_ref[...] = edges_t.astype(bf16)
    after = jnp.minimum(me + 1, cols - 1)

    loads[5].wait()

    def turn_block(b, carry):
        at_ref[b] = a_ref[b].astype(f32).T.astype(bf16)
        return carry

    lax.fori_loop(0, blocks, turn_block, 0, unroll=4)
    loads[6].wait()
    bit = jnp.left_shift(1, lax.broadcasted_iota(i32, (8, 128), 0))

    def open_mask(s, carry):
        for pair in range(8):
            parts = []
            for w in (2 * pair, 2 * pair + 1):
                word = jnp.broadcast_to(w_ref[s, w : w + 1, :], (8, 128))
                parts.append(jnp.where((word & bit) != 0, 1.0, 0.0))
            m_ref[s, 16 * pair : 16 * pair + 16, :] = jnp.concatenate(parts, axis=0).astype(bf16)
        return carry

    cuts = [slots * n // (chips - 1) for n in range(chips)]
    for n in range(chips - 1):
        lax.fori_loop(cuts[n], cuts[n + 1], open_mask, 0, unroll=2)
        sent.append(pass_on(n, r1_ref, g1_send, g1_recv))
    to_scalars.wait()

    def by_lane(x):
        return jnp.sum(x, axis=0, keepdims=True)

    def over_lanes(x):
        return jnp.sum(x, axis=1, keepdims=True)

    sublane = lax.broadcasted_iota(i32, (8, 128), 0)

    def stack(*lines):
        out = jnp.zeros((8, 128), f32)
        for n, line in enumerate(lines):
            out = jnp.where(sublane == n, line, out)
        return out

    def first_half(r_ref):
        def turn(k, squares):
            code = code_sm[0, k]
            item = jnp.minimum(code & 63, blocks - 1)
            s, u = jnp.minimum((code >> 6) & 127, slots - 1), jnp.minimum((code >> 13) & 31, cols)
            scores = jnp.dot(at_ref[item], r_ref[u], preferred_element_type=f32)
            tile = scores.astype(bf16) * m_ref[s]
            t_ref[k] = tile
            square = scores * tile.astype(f32)
            return squares + jnp.sum(square.reshape(-1, 8, 128), axis=0)

        return lax.fori_loop(0, slots, turn, jnp.zeros((8, 128), f32), unroll=UNROLL)

    def second_half():
        def turn(k, carry):
            acc, last = carry
            code = code_sm[0, k]
            item, u = jnp.minimum(code & 63, blocks - 1), code >> 13
            part = jnp.dot(a_ref[item], t_ref[k], preferred_element_type=f32)
            acc = jnp.where(u == last, acc, 0.0) + part
            s_ref[k + 1] = acc
            return acc, u

        start = (jnp.zeros(s_ref.shape[1:], f32), i32(-1))
        lax.fori_loop(0, slots, turn, start, unroll=UNROLL)

    def summed(u):
        return s_ref[jnp.minimum(code_sm[1, u] & 127, slots)]

    def graph(r_ref):
        own, following = r_ref[me], r_ref[after]
        here = here_degree * own.astype(f32)
        here = here - jnp.dot(own, sym_ref[...], preferred_element_type=f32)
        here = here - jnp.dot(following, et_ref[...], preferred_element_type=f32)
        there = there_degree * following.astype(f32)
        there = there - jnp.dot(own, e_ref[...], preferred_element_type=f32)
        form = own.astype(f32) * here + following.astype(f32) * there
        return GRAPH * here, GRAPH * there, GRAPH * by_lane(form)

    def scatter(here, there, x_ref, yp_ref, z_ref, y_ref, xp_send, xp_recv, z_send, z_recv):
        copies = []
        for n, o in enumerate(far + [0]):
            p = chip(o)
            block = p * 2 + 1 - my_core
            value = summed(block) + jnp.where(block == me + 1, there, 0.0)
            x_ref[pl.ds(p, 1)] = value.astype(bf16)[None]
            copies.append(
                remote(x_ref.at[p], yp_ref.at[p], xp_send.at[n], xp_recv.at[p], {"col": partner})
            )
        for n, o in enumerate(far):
            p = chip(o)
            value = summed(p * 2 + my_core)
            arrived(yp_ref.at[p], xp_recv.at[p])
            z_ref[pl.ds(p, 1)] = (value + yp_ref[p].astype(f32)).astype(bf16)[None]
            copies.append(
                remote(
                    z_ref.at[p],
                    y_ref.at[my_chip],
                    z_send.at[n],
                    z_recv.at[my_chip],
                    {"col": p * 2 + my_core},
                )
            )
        arrived(yp_ref.at[my_chip], xp_recv.at[my_chip])
        return summed(me) + here + yp_ref[my_chip].astype(f32), copies

    def total(own, y_ref, z_recv):
        for o in near:
            p = chip(o)
            arrived(y_ref.at[p], z_recv.at[p])
            own = own + y_ref[p].astype(f32)
        return own

    def share(p_ref, value, send, recv):
        p_ref[pl.ds(me, 1)] = value[None]
        return [
            remote(
                p_ref.at[me],
                p_ref.at[me],
                send.at[o],
                recv.at[me],
                {"col": lax.rem(me + o, cols)},
            )
            for o in sorted(range(1, cols), key=lambda o: -min(o, cols - o))
        ]

    def all_shares(p_ref, recv):
        for o in range(1, cols):
            other = lax.rem(me + o, cols)
            arrived(p_ref.at[other], recv.at[other])
        return jnp.sum(p_ref[...], axis=0)

    finish(r1_ref, g1_recv)
    here, there, form = graph(r1_ref)
    form = form + by_lane(first_half(r1_ref)) + RIDGE * by_lane(rhs * rhs)
    sent += share(p1_ref, stack(by_lane(rhs * rhs), form), p1_send, p1_recv)
    second_half()
    own, copies = scatter(
        here, there, x1_ref, yp1_ref, z1_ref, y1_ref, xp1_send, xp1_recv, z1_send, z1_recv
    )
    sent += copies
    line = all_shares(p1_ref, p1_recv)
    norm_line, form_line = line[0:1, :], line[1:2, :]
    norm_row, form_row = over_lanes(norm_line), over_lanes(form_line)
    shift = jnp.where(norm_row > 0.0, form_row / jnp.where(norm_row > 0.0, norm_row, 1.0), 0.0)
    w = total(own, y1_ref, z1_recv) + RIDGE * rhs

    v = w - shift * rhs
    r2_ref[pl.ds(me, 1)] = v.astype(bf16)[None]
    sent += gather(r2_ref, g2_send, g2_recv)
    square = by_lane(w * w)
    for n in range(chips - 1):
        sent.append(pass_on(n, r2_ref, g2_send, g2_recv))
    finish(r2_ref, g2_recv)
    here, there, form = graph(r2_ref)
    form = form + by_lane(first_half(r2_ref)) + RIDGE * by_lane(v * v)
    sent += share(p2_ref, stack(square, form), p2_send, p2_recv)
    second_half()
    own, copies = scatter(
        here, there, x2_ref, yp2_ref, z2_ref, y2_ref, xp2_send, xp2_recv, z2_send, z2_recv
    )
    sent += copies
    line = all_shares(p2_ref, p2_recv)
    square_line, bent_line = line[0:1, :], line[1:2, :]
    cubic_line = bent_line + 2.0 * shift * square_line - shift * shift * form_line
    p3_ref[pl.ds(my_row, 1)] = stack(norm_line, form_line, square_line, cubic_line)[None]
    for o in range(1, rows):
        sent.append(
            remote(
                p3_ref.at[my_row],
                p3_ref.at[my_row],
                p3_send.at[o - 1],
                p3_recv.at[my_row],
                {"row": lax.rem(my_row + o, rows)},
            )
        )
    hv = total(own, y2_ref, z2_recv) + RIDGE * v
    z = hv + shift * w
    for o in range(1, rows):
        other = lax.rem(my_row + o, rows)
        arrived(p3_ref.at[other], p3_recv.at[other])
    sums = over_lanes(jnp.sum(p3_ref[...], axis=0))
    norm0, form1, square1, cubic1 = (sums[n : n + 1, :] for n in range(4))
    alpha1 = norm0 / form1
    norm1 = norm0 - 2.0 * alpha1 * form1 + alpha1 * alpha1 * square1
    more = 1.0 + norm1 / norm0
    curve = more * more * form1 - 2.0 * more * alpha1 * square1 + alpha1 * alpha1 * cubic1
    alpha2 = norm1 / curve
    plus, cross = alpha1 + alpha2 * more, alpha1 * alpha2
    out_ref[0] = (plus - 1.0) * rhs - cross * w
    out_ref[1] = cross * z - plus * w

    for copy in sent:
        copy.wait_send()


def per_device(rows, cols, *args):
    rhs, items, users, slot_items, counts, words, selfs, nexts = args
    slots = users.shape[2]
    blocks, rank, width = items.shape
    chips = cols // 2
    vmem = pl.BlockSpec(memory_space=pltpu.VMEM)
    hbm = pl.BlockSpec(memory_space=pl.ANY)
    dma = pltpu.SemaphoreType.DMA
    half = pltpu.VMEM((chips, rank, width), bf16)
    out = pl.pallas_call(
        functools.partial(kernel, rows, cols),
        out_shape=jax.ShapeDtypeStruct((2, rank, width), f32),
        in_specs=[hbm] * 8,
        out_specs=vmem,
        scratch_shapes=[
            pltpu.VMEM((rank, width), f32),
            pltpu.VMEM((1, slots), i32),
            pltpu.VMEM((1, slots), i32),
            pltpu.VMEM((1, 1), i32),
            pltpu.VMEM((blocks, rank, width), bf16),
            pltpu.VMEM((blocks, width, rank), bf16),
            pltpu.VMEM((slots, width // 8, width), i32),
            pltpu.VMEM((slots, width, width), bf16),
            pltpu.VMEM((slots, width, width), bf16),
            pltpu.VMEM((slots + 1, rank, width), f32),
            pltpu.VMEM((cols + 1, rank, width), bf16),
            pltpu.VMEM((cols + 1, rank, width), bf16),
            *[half] * 8,
            pltpu.VMEM((width, width), i32),
            pltpu.VMEM((width, width), i32),
            pltpu.VMEM((width, width), bf16),
            pltpu.VMEM((width, width), bf16),
            pltpu.VMEM((width, width), bf16),
            pltpu.VMEM((8, 128), i32),
            pltpu.SMEM((8, 128), i32),
            pltpu.VMEM((cols, 8, 128), f32),
            pltpu.VMEM((cols, 8, 128), f32),
            pltpu.VMEM((rows, 8, 128), f32),
            dma((9,)),
            *[dma((cols,))] * 8,
            *[dma((chips,))] * 8,
            dma((rows,)),
            dma((rows,)),
        ],
        compiler_params=pltpu.CompilerParams(collective_id=0, has_side_effects=True),
        name="cg",
    )(*args)
    return out[0:1] + rhs, out[1:2] + rhs


def solution(mesh):
    rows, cols = mesh.shape["row"], mesh.shape["col"]
    user_blocks = P(("row", "col"), None, None)
    return jax.shard_map(
        functools.partial(per_device, rows, cols),
        mesh=mesh,
        in_specs=(
            user_blocks,
            P("col", None, None),
            P("row", "col", None),
            P("row", "col", None),
            P("row", "col"),
            P("row", "col", None, None, None),
            user_blocks,
            user_blocks,
        ),
        out_specs=(user_blocks, user_blocks),
        check_vma=False,
    )
```

time: 76.3 us -> 59.9 us (0.79)
  Pallas kernels: 72.7 us -> 56.9 us
  local copies, waits for them, and re-layouts: 2 us -> 0.01 us
  other arithmetic: 0 us -> 1.41 us
    pallas_call x1, Pallas kernels: 72.7 us -> 56.9 us  [per_device(): pl.pallas_call(functools.partial(kernel, rows, cols), out_shape=jax.Shape...]
    unnamed x4 -> x2, local copies, waits for them, and re-layouts: 2 us -> 0.01 us
    add x0 -> x1, other arithmetic: none -> 1.41 us  [per_device(): return (out[0:1] + rhs, out[1:2] + rhs)]
where the time goes in v2:
time: 59.9 us; the launch traced here: 59.6 us
  Pallas kernels  56.9 us (95%)
  other arithmetic  1.41 us (2%)
  between operations  1.3 us (2%)
    pallas_call x1, Pallas kernels, per_device(): pl.pallas_call(functools.partial(kernel, rows, cols), out_shape=jax.Shape...  56.9 us
    add x1, other arithmetic, per_device(): return (out[0:1] + rhs, out[1:2] + rhs)  1.41 us

profile of v2, /device:TPU:1, one launch (start us, length us, event | category | flops | bytes accessed | tf_op | source)
XLA Modules:
  0.0 59.6 jit_solution(9008255724053779842)
XLA Ops:
  1.3 0.0 copy-start
  1.3 56.9 %cg.1 = f32[2,64,128]{2,1,0:T(8,128)} custom-call(f32[1,64,128]{2,1,0:T(8,128)} %rhs_hbm.1, bf16[64,64,128]{2,1,0:T(8,128)(2,1)} %items_hbm.1, s32[1,1,96]{2,1,0:T(1,128)} %users_hbm.1, s32[1,1,96]{2,1,0:T(1,128)} %slot_items_hbm.1, s32[1,1]{1,0:T(1,128)S(6)} %copy.10.count_hbm, s32[1,1,96,16,128]{4,3,2,1,0:T(8,128)} %words_hbm.1, s32[1,128,128]{2,1,0:T(8,128)} %self_hbm.1, ...), custom_call_target="tpu_custom_call" | custom-call | tf_op jit(solution)/shard_map/cg/pallas_call | solution.py:409
  58.2 0.0 copy-done
  58.2 1.4 %slice_add_fusion = (f32[1,64,128]{2,1,0:T(8,128)}, f32[1,64,128]{2,1,0:T(8,128)}) fusion(f32[1,64,128]{2,1,0:T(8,128)S(1)} %copy-done, f32[2,64,128]{2,1,0:T(8,128)} %cg.1), kind=kLoop, calls=%fused_computation | loop fusion | flops 16384 | bytes 163840 | tf_op jit(solution)/shard_map/add | solution.py:447
Async XLA Ops:
  1.3 56.9 %copy-start = (f32[1,64,128]{2,1,0:T(8,128)S(1)}, f32[1,64,128]{2,1,0:T(8,128)}, u32[]{:S(2)}) copy-start(f32[1,64,128]{2,1,0:T(8,128)} %rhs_hbm.1) | copy-start | bytes 98308

commit v3 on v2

--- a/solution.py
+++ b/solution.py
@@ -9,7 +9,7 @@
 
 GRAPH = 0.01
 RIDGE = 0.5
-UNROLL = 8
+UNROLL = 16
 f32, bf16, i32 = jnp.float32, jnp.bfloat16, jnp.int32
 
 
@@ -233,13 +233,11 @@
     def over_lanes(x):
         return jnp.sum(x, axis=1, keepdims=True)
 
-    sublane = lax.broadcasted_iota(i32, (8, 128), 0)
-
-    def stack(*lines):
-        out = jnp.zeros((8, 128), f32)
-        for n, line in enumerate(lines):
-            out = jnp.where(sublane == n, line, out)
-        return out
+    def pack(a, b):
+        return jnp.where(lane < 64, a + pltpu.roll(a, 64, 1), b + pltpu.roll(b, 64, 1))
+
+    def unpack(line):
+        return over_lanes(jnp.where(lane < 64, line, 0.0)), over_lanes(jnp.where(lane < 64, 0.0, line))
 
     def first_half(r_ref):
         def turn(k, squares):
@@ -267,6 +265,22 @@
         start = (jnp.zeros(s_ref.shape[1:], f32), i32(-1))
         lax.fori_loop(0, slots, turn, start, unroll=UNROLL)
 
+    def halves(r_ref):
+        def turn(k, carry):
+            acc, last = carry
+            code = code_sm[0, k]
+            item = jnp.minimum(code & 63, blocks - 1)
+            s, u = jnp.minimum((code >> 6) & 127, slots - 1), jnp.minimum((code >> 13) & 31, cols)
+            scores = jnp.dot(at_ref[item], r_ref[u], preferred_element_type=f32)
+            tile = scores.astype(bf16) * m_ref[s]
+            part = jnp.dot(a_ref[item], tile, preferred_element_type=f32)
+            acc = jnp.where(u == last, acc, 0.0) + part
+            s_ref[k + 1] = acc
+            return acc, u
+
+        start = (jnp.zeros(s_ref.shape[1:], f32), i32(-1))
+        lax.fori_loop(0, slots, turn, start, unroll=UNROLL)
+
     def summed(u):
         return s_ref[jnp.minimum(code_sm[1, u] & 127, slots)]
 
@@ -280,7 +294,7 @@
         form = own.astype(f32) * here + following.astype(f32) * there
         return GRAPH * here, GRAPH * there, GRAPH * by_lane(form)
 
-    def scatter(here, there, x_ref, yp_ref, z_ref, y_ref, xp_send, xp_recv, z_send, z_recv):
+    def scatter(here, there, meanwhile, x_ref, yp_ref, z_ref, y_ref, xp_send, xp_recv, z_send, z_recv):
         copies = []
         for n, o in enumerate(far + [0]):
             p = chip(o)
@@ -290,6 +304,7 @@
             copies.append(
                 remote(x_ref.at[p], yp_ref.at[p], xp_send.at[n], xp_recv.at[p], {"col": partner})
             )
+        copies += meanwhile()
         for n, o in enumerate(far):
             p = chip(o)
             value = summed(p * 2 + my_core)
@@ -334,17 +349,22 @@
         return jnp.sum(p_ref[...], axis=0)
 
     finish(r1_ref, g1_recv)
-    here, there, form = graph(r1_ref)
-    form = form + by_lane(first_half(r1_ref)) + RIDGE * by_lane(rhs * rhs)
-    sent += share(p1_ref, stack(by_lane(rhs * rhs), form), p1_send, p1_recv)
-    second_half()
+    here, there, near_form = graph(r1_ref)
+    halves(r1_ref)
+
+    def meanwhile():
+        norm = by_lane(rhs * rhs)
+        form = jnp.zeros(rhs.shape, f32)
+        for u in range(cols):
+            form = form + r1_ref[u].astype(f32) * summed(u)
+        form = by_lane(form) + near_form + RIDGE * norm
+        return share(p1_ref, pack(norm, form), p1_send, p1_recv)
+
     own, copies = scatter(
-        here, there, x1_ref, yp1_ref, z1_ref, y1_ref, xp1_send, xp1_recv, z1_send, z1_recv
+        here, there, meanwhile, x1_ref, yp1_ref, z1_ref, y1_ref, xp1_send, xp1_recv, z1_send, z1_recv
     )
     sent += copies
-    line = all_shares(p1_ref, p1_recv)
-    norm_line, form_line = line[0:1, :], line[1:2, :]
-    norm_row, form_row = over_lanes(norm_line), over_lanes(form_line)
+    norm_row, form_row = unpack(all_shares(p1_ref, p1_recv))
     shift = jnp.where(norm_row > 0.0, form_row / jnp.where(norm_row > 0.0, norm_row, 1.0), 0.0)
     w = total(own, y1_ref, z1_recv) + RIDGE * rhs
 
@@ -357,16 +377,17 @@
     finish(r2_ref, g2_recv)
     here, there, form = graph(r2_ref)
     form = form + by_lane(first_half(r2_ref)) + RIDGE * by_lane(v * v)
-    sent += share(p2_ref, stack(square, form), p2_send, p2_recv)
+    sent += share(p2_ref, pack(square, form), p2_send, p2_recv)
     second_half()
     own, copies = scatter(
-        here, there, x2_ref, yp2_ref, z2_ref, y2_ref, xp2_send, xp2_recv, z2_send, z2_recv
+        here, there, list, x2_ref, yp2_ref, z2_ref, y2_ref, xp2_send, xp2_recv, z2_send, z2_recv
     )
     sent += copies
-    line = all_shares(p2_ref, p2_recv)
-    square_line, bent_line = line[0:1, :], line[1:2, :]
-    cubic_line = bent_line + 2.0 * shift * square_line - shift * shift * form_line
-    p3_ref[pl.ds(my_row, 1)] = stack(norm_line, form_line, square_line, cubic_line)[None]
+    square_row, bent_row = unpack(all_shares(p2_ref, p2_recv))
+    cubic_row = bent_row + 2.0 * shift * square_row - shift * shift * form_row
+    line = jnp.where(lane < 64, square_row, cubic_row)
+    line = jnp.where(lane == 0, norm_row, jnp.where(lane == 1, form_row, line))
+    p3_ref[pl.ds(my_row, 1)] = line[None]
     for o in range(1, rows):
         sent.append(
             remote(
@@ -382,8 +403,10 @@
     for o in range(1, rows):
         other = lax.rem(my_row + o, rows)
         arrived(p3_ref.at[other], p3_recv.at[other])
-    sums = over_lanes(jnp.sum(p3_ref[...], axis=0))
-    norm0, form1, square1, cubic1 = (sums[n : n + 1, :] for n in range(4))
+    line = jnp.sum(p3_ref[...], axis=0)
+    norm0, form1, square1, cubic1 = (
+        over_lanes(jnp.where(lane == n, line, 0.0)) for n in (0, 1, 2, 64)
+    )
     alpha1 = norm0 / form1
     norm1 = norm0 - 2.0 * alpha1 * form1 + alpha1 * alpha1 * square1
     more = 1.0 + norm1 / norm0
@@ -403,7 +426,7 @@
     blocks, rank, width = items.shape
     chips = cols // 2
     vmem = pl.BlockSpec(memory_space=pltpu.VMEM)
-    hbm = pl.BlockSpec(memory_space=pl.ANY)
+    hbm = pl.BlockSpec(memory_space=pltpu.HBM)
     dma = pltpu.SemaphoreType.DMA
     half = pltpu.VMEM((chips, rank, width), bf16)
     out = pl.pallas_call(
@@ -432,9 +455,9 @@
             pltpu.VMEM((width, width), bf16),
             pltpu.VMEM((8, 128), i32),
             pltpu.SMEM((8, 128), i32),
-            pltpu.VMEM((cols, 8, 128), f32),
-            pltpu.VMEM((cols, 8, 128), f32),
-            pltpu.VMEM((rows, 8, 128), f32),
+            pltpu.VMEM((cols, 1, 128), f32),
+            pltpu.VMEM((cols, 1, 128), f32),
+            pltpu.VMEM((rows, 1, 128), f32),
             dma((9,)),
             *[dma((cols,))] * 8,
             *[dma((chips,))] * 8,

time: 59.9 us -> 55.3 us (0.923)
  Pallas kernels: 56.9 us -> 52.3 us
    pallas_call x1, Pallas kernels: 56.9 us -> 52.3 us  [per_device(): pl.pallas_call(functools.partial(kernel, rows, cols), out_shape=jax.Shape...]
where the time goes in v3:
time: 55.3 us; the launch traced here: 55 us
  Pallas kernels  52.3 us (95%)
  other arithmetic  1.41 us (3%)
  between operations  1.3 us (2%)
    pallas_call x1, Pallas kernels, per_device(): pl.pallas_call(functools.partial(kernel, rows, cols), out_shape=jax.Shape...  52.3 us
    add x1, other arithmetic, per_device(): return (out[0:1] + rhs, out[1:2] + rhs)  1.41 us

profile of v3, /device:TPU:1, one launch (start us, length us, event | category | flops | bytes accessed | tf_op | source)
XLA Modules:
  0.0 55.0 jit_solution(12834854717847510056)
XLA Ops:
  1.3 0.0 copy-start
  1.3 52.3 %cg.1 = f32[2,64,128]{2,1,0:T(8,128)} custom-call(f32[1,64,128]{2,1,0:T(8,128)} %rhs_hbm.1, bf16[64,64,128]{2,1,0:T(8,128)(2,1)} %items_hbm.1, s32[1,1,96]{2,1,0:T(1,128)} %users_hbm.1, s32[1,1,96]{2,1,0:T(1,128)} %slot_items_hbm.1, s32[1,1]{1,0:T(1,128)S(6)} %copy.10.count_hbm, s32[1,1,96,16,128]{4,3,2,1,0:T(8,128)} %words_hbm.1, s32[1,128,128]{2,1,0:T(8,128)} %self_hbm.1, ...), custom_call_target="tpu_custom_call" | custom-call | tf_op jit(solution)/shard_map/cg/pallas_call | solution.py:432
  53.6 0.0 copy-done
  53.6 1.4 %slice_add_fusion = (f32[1,64,128]{2,1,0:T(8,128)}, f32[1,64,128]{2,1,0:T(8,128)}) fusion(f32[1,64,128]{2,1,0:T(8,128)S(1)} %copy-done, f32[2,64,128]{2,1,0:T(8,128)} %cg.1), kind=kLoop, calls=%fused_computation | loop fusion | flops 16384 | bytes 163840 | tf_op jit(solution)/shard_map/add | solution.py:470
Async XLA Ops:
  1.3 52.3 %copy-start = (f32[1,64,128]{2,1,0:T(8,128)S(1)}, f32[1,64,128]{2,1,0:T(8,128)}, u32[]{:S(2)}) copy-start(f32[1,64,128]{2,1,0:T(8,128)} %rhs_hbm.1) | copy-start | bytes 98308

commit v4 on v3

--- a/solution.py
+++ b/solution.py
@@ -9,7 +9,7 @@
 
 GRAPH = 0.01
 RIDGE = 0.5
-UNROLL = 16
+UNROLL = 48
 f32, bf16, i32 = jnp.float32, jnp.bfloat16, jnp.int32
 
 

time: 55.3 us -> 53.6 us (0.969)
  Pallas kernels: 52.3 us -> 50.6 us
    pallas_call x1, Pallas kernels: 52.3 us -> 50.6 us  [per_device(): pl.pallas_call(functools.partial(kernel, rows, cols), out_shape=jax.Shape...]
where the time goes in v4:
time: 53.6 us; the launch traced here: 53.4 us
  Pallas kernels  50.6 us (94%)
  other arithmetic  1.41 us (3%)
  between operations  1.3 us (2%)
    pallas_call x1, Pallas kernels, per_device(): pl.pallas_call(functools.partial(kernel, rows, cols), out_shape=jax.Shape...  50.6 us
    add x1, other arithmetic, per_device(): return (out[0:1] + rhs, out[1:2] + rhs)  1.41 us

profile of v4, /device:TPU:1, one launch (start us, length us, event | category | flops | bytes accessed | tf_op | source)
XLA Modules:
  0.0 53.4 jit_solution(18420535260872998471)
XLA Ops:
  1.3 0.0 copy-start
  1.3 50.6 %cg.1 = f32[2,64,128]{2,1,0:T(8,128)} custom-call(f32[1,64,128]{2,1,0:T(8,128)} %rhs_hbm.1, bf16[64,64,128]{2,1,0:T(8,128)(2,1)} %items_hbm.1, s32[1,1,96]{2,1,0:T(1,128)} %users_hbm.1, s32[1,1,96]{2,1,0:T(1,128)} %slot_items_hbm.1, s32[1,1]{1,0:T(1,128)S(6)} %copy.10.count_hbm, s32[1,1,96,16,128]{4,3,2,1,0:T(8,128)} %words_hbm.1, s32[1,128,128]{2,1,0:T(8,128)} %self_hbm.1, ...), custom_call_target="tpu_custom_call" | custom-call | tf_op jit(solution)/shard_map/cg/pallas_call | solution.py:432
  51.9 0.0 copy-done
  51.9 1.4 %slice_add_fusion = (f32[1,64,128]{2,1,0:T(8,128)}, f32[1,64,128]{2,1,0:T(8,128)}) fusion(f32[1,64,128]{2,1,0:T(8,128)S(1)} %copy-done, f32[2,64,128]{2,1,0:T(8,128)} %cg.1), kind=kLoop, calls=%fused_computation | loop fusion | flops 16384 | bytes 163840 | tf_op jit(solution)/shard_map/add | solution.py:470
Async XLA Ops:
  1.3 50.7 %copy-start = (f32[1,64,128]{2,1,0:T(8,128)S(1)}, f32[1,64,128]{2,1,0:T(8,128)}, u32[]{:S(2)}) copy-start(f32[1,64,128]{2,1,0:T(8,128)} %rhs_hbm.1) | copy-start | bytes 98308

commit v5 on v4

--- a/solution.py
+++ b/solution.py
@@ -400,6 +400,8 @@
         )
     hv = total(own, y2_ref, z2_recv) + RIDGE * v
     z = hv + shift * w
+    for copy in sent:
+        copy.wait_send()
     for o in range(1, rows):
         other = lax.rem(my_row + o, rows)
         arrived(p3_ref.at[other], p3_recv.at[other])
@@ -415,9 +417,6 @@
     plus, cross = alpha1 + alpha2 * more, alpha1 * alpha2
     out_ref[0] = (plus - 1.0) * rhs - cross * w
     out_ref[1] = cross * z - plus * w
-
-    for copy in sent:
-        copy.wait_send()
 
 
 def per_device(rows, cols, *args):

time: 53.6 us -> 53.5 us (level)
  no operation moved by 1% of the time
where the time goes in v5:
time: 53.5 us; the launch traced here: 53.2 us
  Pallas kernels  50.5 us (94%)
  other arithmetic  1.41 us (3%)
  between operations  1.3 us (2%)
    pallas_call x1, Pallas kernels, per_device(): pl.pallas_call(functools.partial(kernel, rows, cols), out_shape=jax.Shape...  50.5 us
    add x1, other arithmetic, per_device(): return (out[0:1] + rhs, out[1:2] + rhs)  1.41 us

profile of v5, /device:TPU:1, one launch (start us, length us, event | category | flops | bytes accessed | tf_op | source)
XLA Modules:
  0.0 53.2 jit_solution(9925613130595647661)
XLA Ops:
  1.3 0.0 copy-start
  1.3 50.5 %cg.1 = f32[2,64,128]{2,1,0:T(8,128)} custom-call(f32[1,64,128]{2,1,0:T(8,128)} %rhs_hbm.1, bf16[64,64,128]{2,1,0:T(8,128)(2,1)} %items_hbm.1, s32[1,1,96]{2,1,0:T(1,128)} %users_hbm.1, s32[1,1,96]{2,1,0:T(1,128)} %slot_items_hbm.1, s32[1,1]{1,0:T(1,128)S(6)} %copy.10.count_hbm, s32[1,1,96,16,128]{4,3,2,1,0:T(8,128)} %words_hbm.1, s32[1,128,128]{2,1,0:T(8,128)} %self_hbm.1, ...), custom_call_target="tpu_custom_call" | custom-call | tf_op jit(solution)/shard_map/cg/pallas_call | solution.py:431
  51.7 0.0 copy-done
  51.8 1.4 %slice_add_fusion = (f32[1,64,128]{2,1,0:T(8,128)}, f32[1,64,128]{2,1,0:T(8,128)}) fusion(f32[1,64,128]{2,1,0:T(8,128)S(1)} %copy-done, f32[2,64,128]{2,1,0:T(8,128)} %cg.1), kind=kLoop, calls=%fused_computation | loop fusion | flops 16384 | bytes 163840 | tf_op jit(solution)/shard_map/add | solution.py:469
Async XLA Ops:
  1.3 50.5 %copy-start = (f32[1,64,128]{2,1,0:T(8,128)S(1)}, f32[1,64,128]{2,1,0:T(8,128)}, u32[]{:S(2)}) copy-start(f32[1,64,128]{2,1,0:T(8,128)} %rhs_hbm.1) | copy-start | bytes 98308
